TPU v7x, 512 devices: a whole 4x4x16 slice. The times are simulated.
512 devices in a mesh: tm: 16 (over z), det: 32 (over y, x, core).
Axes of the slice: x: 4, y: 4, z: 16, core: 2. Of those that a mesh axis runs over, the one named last changes fastest.
Arguments:
- noise: float32 [512, 65536], P('det', 'tm'), may hold values from -6 to 6
- factor: float32 [32, 512, 512], P('det', 'tm'), may hold values from -8 to 8, as said below
Outputs:
- correlated: float32 [512, 65536], P('det', 'tm')
Inputs may be any that keep to these rules, and one draw needn't show every extreme that they name: factor[b] is lower triangular with a positive diagonal, and factor[b] equals factor[31 - b].
All inputs are finite; a program needn't handle non-finite values.
Results may differ from a plain program's by a relative error of at most 0.00007.
Values sent between devices are 32-bit elements; how exact they have to be, the bound alone decides.
A program may use at most 64 MiB of HBM per device.

v0:
```python
import math

import jax
import jax.numpy as jnp
import numpy as np
from jax import lax
from jax.experimental import pallas as pl
from jax.experimental.pallas import tpu as pltpu
from jax.sharding import PartitionSpec as P

MESH = pl.DeviceIdType.MESH
f32, bf16 = jnp.float32, jnp.bfloat16

PLANES = 16
GROUPS = 32
LANES = 128
ROWS = 512
DETS = 512
TOTAL = 65536


def split(values):
    high = values.astype(bf16)
    return high, (values - high.astype(f32)).astype(bf16)


def table_parts(table):
    high = table.astype(bf16)
    return high, (table - high.astype(np.float64)).astype(bf16)


def make_tables():
    q = np.arange(256)[:, None] + 0.5
    first = 2.0 * math.pi / 512 * (q * np.arange(512)[None, :])
    first = np.concatenate([np.cos(first), -np.sin(first)], axis=0)
    turn = 2.0 * math.pi / TOTAL * (q * np.arange(LANES)[None, :])
    pair = np.arange(16)[:, None]
    place = np.arange(4)[None, :]
    m = np.concatenate([4 * pair + place, 4 * (31 - pair) + place], axis=1)
    second = 2.0 * math.pi / LANES * ((m[:, :, None] * np.arange(LANES)) % LANES)
    cosines, sines = np.cos(second), np.sin(second)
    real_rows = np.concatenate([cosines, sines], axis=2)
    imag_rows = np.concatenate([-sines, cosines], axis=2)
    second = np.concatenate([real_rows, imag_rows], axis=1).reshape(256, 256)
    return (
        *table_parts(first),
        *table_parts(second),
        np.cos(turn).astype(np.float32),
        np.sin(turn).astype(np.float32),
    )


def product(left, right, dims):
    numbers = ((dims[:1], dims[1:]), ((), ()))
    total = None
    for a, b in ((0, 1), (1, 0), (0, 0)):
        term = lax.dot_general(left[a], right[b], numbers, preferred_element_type=f32)
        total = term if total is None else total + term
    return total


def rows_at(index, count):
    return pl.ds(pl.multiple_of(index * count, count), count)


def away(step, count):
    return count // 2 + (step + 1) // 2 * (1 - 2 * (step % 2))


class Exchange:
    def __init__(self, axis, count, rows, source, target, send, recv):
        self.axis, self.count, self.rows = axis, count, rows
        self.source, self.target, self.send, self.recv = source, target, send, recv

    def copy(self, peer, source_block, target_block, slot):
        return pltpu.make_async_remote_copy(
            src_ref=self.source.at[rows_at(source_block, self.rows)],
            dst_ref=self.target.at[rows_at(target_block, self.rows)],
            send_sem=self.send.at[peer],
            recv_sem=self.recv.at[slot],
            device_id={self.axis: peer},
            device_id_type=MESH,
        )

    def each(self, action):
        me = lax.axis_index(self.axis)

        def step(k, carry):
            action(me, lax.rem(me + away(k, self.count), self.count))
            return carry

        lax.fori_loop(0, self.count - 1, step, 0)

    def start(self, own=True):
        self.each(lambda me, peer: self.copy(peer, peer if own else me, me, me).start())
        if own:
            me = lax.axis_index(self.axis)
            here = rows_at(me, self.rows)
            self.target[here] = self.source[here]

    def wait_recv(self):
        self.each(lambda me, peer: self.copy(peer, me, peer, peer).wait_recv())

    def wait_send(self):
        self.each(lambda me, peer: self.copy(peer, peer, me, me).wait_send())


def kernel(
    noise, factor, first_high, first_low, second_high, second_low, cosines, sines, out,
    samples, x0, x1, x2, x3, x4, x5, x6, x7, x8, x9, x10, x11, flat, gathered, factor_high, factor_low,
    t_first_high, t_first_low, t_second_high, t_second_low, t_cos, t_sin,
    z_send, z_recv, d_send, d_recv, f_send, f_recv, part_send, part_recv, local_sem,
):
    plane = lax.axis_index("tm")
    group = lax.axis_index("det")
    upper = group // 16
    pair = group + upper * (31 - 2 * group)
    part_to = (pair, 2 * plane + upper)
    odd = lax.rem(group, 2)
    part_from = (group // 2, plane + odd * (31 - 2 * plane))
    stays = jnp.logical_and(part_to[0] == plane, part_to[1] == group)

    loads = [pltpu.make_async_copy(noise, samples, local_sem.at[0])]
    tables = (
        (first_high, t_first_high), (first_low, t_first_low), (second_high, t_second_high),
        (second_low, t_second_low), (cosines, t_cos), (sines, t_sin),
    )
    for n, (source, target) in enumerate(tables):
        loads.append(pltpu.make_async_copy(source, target, local_sem.at[n + 1]))
    for load in loads:
        load.start()

    barrier = pltpu.get_barrier_semaphore()

    def greet_planes(k, carry):
        peer = lax.rem(plane + away(k, PLANES), PLANES)
        pl.semaphore_signal(barrier, inc=1, device_id={"tm": peer}, device_id_type=MESH)
        return carry

    def greet_groups(k, carry):
        peer = lax.rem(group + away(k, GROUPS), GROUPS)
        pl.semaphore_signal(barrier, inc=1, device_id={"det": peer}, device_id_type=MESH)
        return carry

    lax.fori_loop(0, PLANES - 1, greet_planes, 0)
    lax.fori_loop(0, GROUPS - 1, greet_groups, 0)

    @pl.when(jnp.logical_not(stays))
    def _():
        for other in (part_to, part_from):
            pl.semaphore_signal(
                barrier, inc=1, device_id={"tm": other[0], "det": other[1]}, device_id_type=MESH
            )

    loads[0].wait()
    for j in range(32):
        x0[pl.ds(j, PLANES, stride=32), :] = samples[:, LANES * j : LANES * (j + 1)]

    @pl.when(stays)
    def _():
        pl.semaphore_wait(barrier, PLANES + GROUPS - 2)

    @pl.when(jnp.logical_not(stays))
    def _():
        pl.semaphore_wait(barrier, PLANES + GROUPS)

    def planes(n, source, target):
        return Exchange("tm", PLANES, 32, source, target, z_send.at[n], z_recv.at[n])

    def groups(n, source, target):
        return Exchange("det", GROUPS, 16, source, target, d_send.at[n], d_recv.at[n])

    to_detector = planes(0, x0, x1)
    to_detector.start()

    part = factor.at[0, pl.ds(pl.multiple_of(16 * upper, 16), 16)]
    part_copy = pltpu.make_async_remote_copy(
        src_ref=part,
        dst_ref=gathered.at[rows_at(part_to[1], 16)],
        send_sem=part_send,
        recv_sem=part_recv,
        device_id={"tm": part_to[0], "det": part_to[1]},
        device_id_type=MESH,
    )
    part_stays = pltpu.make_async_copy(part, gathered.at[rows_at(part_to[1], 16)], part_recv)

    @pl.when(jnp.logical_not(stays))
    def _():
        part_copy.start()
        pltpu.make_async_remote_copy(
            src_ref=part,
            dst_ref=gathered.at[rows_at(group, 16)],
            send_sem=part_send,
            recv_sem=part_recv,
            device_id={"tm": part_from[0], "det": part_from[1]},
            device_id_type=MESH,
        ).wait_recv()

    @pl.when(stays)
    def _():
        part_stays.start()
        part_stays.wait()

    factor_rows = Exchange("det", GROUPS, 16, gathered, gathered, f_send, f_recv)
    factor_rows.start(own=False)

    for load in loads[1:]:
        load.wait()
    first = (t_first_high[...], t_first_low[...])
    to_detector.wait_recv()

    samples_of = split(x1[...])
    spectrum = product(first, samples_of, (1, 0))
    real, imag = spectrum[:256], spectrum[256:]
    turned = jnp.concatenate(
        [real * t_cos[...] + imag * t_sin[...], imag * t_cos[...] - real * t_sin[...]], axis=1
    )
    bins = product((t_second_high[...], t_second_low[...]), split(turned), (1, 1))
    for p in range(PLANES):
        for half in range(2):
            x2[32 * p + 16 * half : 32 * p + 16 * half + 16, :] = bins[
                16 * p : 16 * p + 16, LANES * half : LANES * half + LANES
            ]

    to_pair = planes(1, x2, x3)
    to_pair.start()
    factor_rows.wait_recv()
    high, low = split(gathered[...])
    factor_high[...] = high
    factor_low[...] = low
    to_pair.wait_recv()

    for g in range(GROUPS):
        x4[16 * g : 16 * g + 16, :] = x3[pl.ds(g, PLANES, stride=GROUPS), :]
    to_bins = groups(0, x4, x5)
    to_bins.start()
    to_bins.wait_recv()

    x6[...] = product((factor_high[...], factor_low[...]), split(x5[...]), (1, 0))

    from_bins = groups(1, x6, x7)
    from_bins.start()
    from_bins.wait_recv()
    for p in range(PLANES):
        x8[32 * p : 32 * p + 32, :] = x7[pl.ds(p, GROUPS, stride=PLANES), :]

    from_pair = planes(2, x8, x9)
    from_pair.start()
    from_pair.wait_recv()

    for p in range(PLANES):
        for half in range(2):
            flat[16 * p : 16 * p + 16, LANES * half : LANES * half + LANES] = x9[
                32 * p + 16 * half : 32 * p + 16 * half + 16, :
            ]
    back = product(split(flat[...]), (t_second_high[...], t_second_low[...]), (0, 0))
    real, imag = back[:, :LANES], back[:, LANES:]
    turned = jnp.concatenate(
        [real * t_cos[...] - imag * t_sin[...], imag * t_cos[...] + real * t_sin[...]], axis=0
    )
    x10[...] = product(first, split(turned), (0, 0)) * (2.0 / TOTAL)

    to_block = planes(3, x10, x11)
    to_block.start()
    to_block.wait_recv()
    for j in range(32):
        out[:, LANES * j : LANES * (j + 1)] = x11[pl.ds(j, PLANES, stride=32), :]

    @pl.when(jnp.logical_not(stays))
    def _():
        part_copy.wait_send()

    factor_rows.wait_send()
    for exchange in (to_detector, to_pair, to_bins, from_bins, from_pair, to_block):
        exchange.wait_send()


def local(noise, factor):
    any_space = pl.BlockSpec(memory_space=pl.ANY)
    block = pltpu.VMEM((ROWS, LANES), f32)
    return pl.pallas_call(
        kernel,
        out_shape=jax.ShapeDtypeStruct((PLANES, ROWS * LANES // PLANES), f32),
        in_specs=[any_space] * 8,
        out_specs=pl.BlockSpec(memory_space=pltpu.VMEM),
        scratch_shapes=[
            pltpu.VMEM((PLANES, ROWS * LANES // PLANES), f32),
            *[block] * 12,
            pltpu.VMEM((256, 256), f32),
            pltpu.VMEM((DETS, DETS), f32),
            pltpu.VMEM((DETS, DETS), bf16),
            pltpu.VMEM((DETS, DETS), bf16),
            pltpu.VMEM((512, 512), bf16),
            pltpu.VMEM((512, 512), bf16),
            pltpu.VMEM((256, 256), bf16),
            pltpu.VMEM((256, 256), bf16),
            pltpu.VMEM((256, LANES), f32),
            pltpu.VMEM((256, LANES), f32),
            pltpu.SemaphoreType.DMA((4, PLANES)),
            pltpu.SemaphoreType.DMA((4, PLANES)),
            pltpu.SemaphoreType.DMA((2, GROUPS)),
            pltpu.SemaphoreType.DMA((2, GROUPS)),
            pltpu.SemaphoreType.DMA((GROUPS,)),
            pltpu.SemaphoreType.DMA((GROUPS,)),
            pltpu.SemaphoreType.DMA,
            pltpu.SemaphoreType.DMA,
            pltpu.SemaphoreType.DMA((8,)),
        ],
        compiler_params=pltpu.CompilerParams(collective_id=0, has_side_effects=True),
        name="mix",
    )(noise, factor, *make_tables())


def solution(mesh):
    in_specs = (P("det", "tm"), P("det", "tm", None))
    return jax.shard_map(local, mesh=mesh, in_specs=in_specs, out_specs=P("det", "tm"), check_vma=False)
```

profile of v0, /device:TPU:24, one launch (start us, length us, event | category | flops | bytes accessed | tf_op | source)
XLA Modules:
  0.0 100.5 jit_solution(10205848921781791556)
XLA Ops:
  0.0 98.8 %mix.1 = f32[16,4096]{1,0:T(8,128)} custom-call(f32[16,4096]{1,0:T(8,128)} %noise.1, f32[1,32,512]{2,1,0:T(8,128)} %factor.1, bf16[512,512]{1,0:T(8,128)(2,1)} %constant.12.clone.first_high, bf16[512,512]{1,0:T(8,128)(2,1)} %constant.13.clone.first_low, bf16[256,256]{1,0:T(8,128)(2,1)} %constant.14.clone.second_high, ...), custom_call_target="tpu_custom_call" | custom-call | tf_op jit(solution)/shard_map/mix/pallas_call | solution.py:281
  98.8 1.7 %copy.10 = f32[16,4096]{1,0:T(8,128)} copy(f32[16,4096]{1,0:T(8,128)} %mix.1) | data formatting | bytes 524288
where the time goes:
time: 102 us; the launch traced here: 101 us
  Pallas kernels  98.8 us (97%)
  local copies, waits for them, and re-layouts  1.67 us (2%)
    pallas_call x1, Pallas kernels, local(): pl.pallas_call(kernel, out_shape=jax.ShapeDtypeStruct((PLANES, ROWS * LAN...  98.8 us

commit v1 on v0

v1 whole, which is shorter than its diff:
```python
import math

import jax
import jax.numpy as jnp
import numpy as np
from jax import lax
from jax.experimental import pallas as pl
from jax.experimental.pallas import tpu as pltpu
from jax.sharding import PartitionSpec as P

MESH = pl.DeviceIdType.MESH
f32, bf16 = jnp.float32, jnp.bfloat16

PLANES = 16
GROUPS = 32
LANES = 128
ROWS = 512
DETS = 512
TOTAL = 65536
CHUNKS = 4


def split(values):
    high = values.astype(bf16)
    return high, (values - high.astype(f32)).astype(bf16)


def table_parts(table):
    high = table.astype(bf16)
    return high, (table - high.astype(np.float64)).astype(bf16)


def make_tables():
    q = np.arange(256)[:, None] + 0.5
    first = 2.0 * math.pi / 512 * (q * np.arange(512)[None, :])
    first = np.concatenate([np.cos(first), -np.sin(first)], axis=0)
    turn = 2.0 * math.pi / TOTAL * (q * np.arange(LANES)[None, :])
    pair = np.arange(16)[:, None]
    place = np.arange(4)[None, :]
    m = np.concatenate([4 * pair + place, 4 * (31 - pair) + place], axis=1)
    second = 2.0 * math.pi / LANES * ((m[:, :, None] * np.arange(LANES)) % LANES)
    cosines, sines = np.cos(second), np.sin(second)
    real_rows = np.concatenate([cosines, sines], axis=2)
    imag_rows = np.concatenate([-sines, cosines], axis=2)
    second = np.concatenate([real_rows, imag_rows], axis=1).reshape(256, 256)
    return (
        *table_parts(first),
        *table_parts(second),
        np.cos(turn).astype(np.float32),
        np.sin(turn).astype(np.float32),
    )


def product(left, right, dims):
    numbers = ((dims[:1], dims[1:]), ((), ()))
    total = None
    for a, b in ((0, 1), (1, 0), (0, 0)):
        term = lax.dot_general(left[a], right[b], numbers, preferred_element_type=f32)
        total = term if total is None else total + term
    return total


def rows_at(index, count):
    return pl.ds(pl.multiple_of(index * count, count), count)


def away(step, count):
    return count // 2 + (step + 1) // 2 * (1 - 2 * (step % 2))


class Exchange:
    def __init__(self, axis, count, rows, chunks, source, target, send, recv):
        self.axis, self.count, self.rows, self.chunks = axis, count, rows, chunks
        self.source, self.target, self.send, self.recv = source, target, send, recv

    def block(self, ref, index, chunk):
        return ref.at[rows_at(index * self.chunks + chunk, self.rows)]

    def copy(self, peer, source_block, target_block, slot, chunk):
        return pltpu.make_async_remote_copy(
            src_ref=self.block(self.source, source_block, chunk),
            dst_ref=self.block(self.target, target_block, chunk),
            send_sem=self.send.at[peer, chunk],
            recv_sem=self.recv.at[slot, chunk],
            device_id={self.axis: peer},
            device_id_type=MESH,
        )

    def each(self, action):
        me = lax.axis_index(self.axis)

        def step(k, carry):
            action(me, lax.rem(me + away(k, self.count), self.count))
            return carry

        lax.fori_loop(0, self.count - 1, step, 0, unroll=True)

    def start(self, chunk=0):
        self.each(lambda me, peer: self.copy(peer, peer, me, me, chunk).start())
        me = lax.axis_index(self.axis)
        here = rows_at(me * self.chunks + chunk, self.rows)
        self.target[here] = self.source[here]

    def wait_recv(self, chunk=0):
        self.each(lambda me, peer: self.copy(peer, me, peer, peer, chunk).wait_recv())

    def wait_send(self):
        for chunk in range(self.chunks):
            self.each(lambda me, peer: self.copy(peer, peer, me, me, chunk).wait_send())


def kernel(
    noise, factor, first_high, first_low, second_high, second_low, cosines, sines, out,
    samples, x0, x1, x2, x3, x4, x5, x6, x7, x8, x9, x10, x11, flat, turned_high, turned_low, gathered, factor_high, factor_low,
    t_first_high, t_first_low, t_second_high, t_second_low, t_cos, t_sin,
    z_send, z_recv, c_send, c_recv, d_send, d_recv, f_send, f_recv, part_send, part_recv, local_sem,
):
    plane = lax.axis_index("tm")
    group = lax.axis_index("det")
    upper = group // 16
    core = lax.rem(group, 2)
    chip = group // 2
    kind = lax.rem(group, CHUNKS)
    pair = group + upper * (31 - 2 * group)
    part_to = (pair, 2 * plane + upper)
    part_from = (chip, plane + core * (31 - 2 * plane))
    stays = jnp.logical_and(part_to[0] == plane, part_to[1] == group)
    leaves = jnp.logical_not(stays)

    loads = [pltpu.make_async_copy(noise, samples, local_sem.at[0])]
    tables = (
        (first_high, t_first_high), (first_low, t_first_low), (second_high, t_second_high),
        (second_low, t_second_low), (cosines, t_cos), (sines, t_sin),
    )
    for n, (source, target) in enumerate(tables):
        loads.append(pltpu.make_async_copy(source, target, local_sem.at[n + 1]))
    loads[0].start()

    barrier = pltpu.get_barrier_semaphore()

    def greet_planes(k, carry):
        peer = lax.rem(plane + away(k, PLANES), PLANES)
        pl.semaphore_signal(barrier, inc=1, device_id={"tm": peer}, device_id_type=MESH)
        return carry

    def greet_groups(k, carry):
        peer = lax.rem(group + away(k, GROUPS), GROUPS)
        pl.semaphore_signal(barrier, inc=1, device_id={"det": peer}, device_id_type=MESH)
        return carry

    lax.fori_loop(0, PLANES - 1, greet_planes, 0, unroll=True)

    @pl.when(leaves)
    def _():
        for other in (part_to, part_from):
            pl.semaphore_signal(
                barrier, inc=1, device_id={"tm": other[0], "det": other[1]}, device_id_type=MESH
            )

    lax.fori_loop(0, GROUPS - 1, greet_groups, 0, unroll=True)
    for load in loads[1:]:
        load.start()

    loads[0].wait()
    for j in range(32):
        x0[pl.ds(j, PLANES, stride=32), :] = samples[:, LANES * j : LANES * (j + 1)]

    @pl.when(stays)
    def _():
        pl.semaphore_wait(barrier, PLANES + GROUPS - 2)

    @pl.when(leaves)
    def _():
        pl.semaphore_wait(barrier, PLANES + GROUPS)

    part = factor.at[0, pl.ds(pl.multiple_of(16 * upper, 16), 16)]

    def factor_block(index):
        return gathered.at[index // 2, pl.ds(pl.multiple_of(16 * lax.rem(index, 2), 16), 16)]

    part_copy = pltpu.make_async_remote_copy(
        src_ref=part,
        dst_ref=factor_block(part_to[1]),
        send_sem=part_send.at[0],
        recv_sem=part_recv.at[0],
        device_id={"tm": part_to[0], "det": part_to[1]},
        device_id_type=MESH,
    )
    part_stays = pltpu.make_async_copy(part, factor_block(group), part_recv.at[0])

    @pl.when(leaves)
    def _():
        part_copy.start()

    @pl.when(stays)
    def _():
        part_stays.start()

    to_detector = Exchange("tm", PLANES, 32, 1, x0, x1, z_send.at[0], z_recv.at[0])
    to_detector.start()

    def chip_copy(other, block):
        return pltpu.make_async_remote_copy(
            src_ref=factor_block(2 * block + core),
            dst_ref=factor_block(2 * block + core),
            send_sem=f_send.at[other],
            recv_sem=f_recv.at[block],
            device_id={"det": 2 * other + core},
            device_id_type=MESH,
        )

    def each_chip(action):
        def step(k, carry):
            action(lax.rem(chip + away(k, 16), 16))
            return carry

        lax.fori_loop(0, 15, step, 0, unroll=True)

    def half_of(index):
        return gathered.at[:, pl.ds(pl.multiple_of(16 * index, 16), 16)]

    def core_copy(half):
        return pltpu.make_async_remote_copy(
            src_ref=half_of(half),
            dst_ref=half_of(half),
            send_sem=part_send.at[1],
            recv_sem=part_recv.at[1],
            device_id={"det": group + 1 - 2 * core},
            device_id_type=MESH,
        )

    @pl.when(leaves)
    def _():
        pltpu.make_async_remote_copy(
            src_ref=part,
            dst_ref=factor_block(group),
            send_sem=part_send.at[0],
            recv_sem=part_recv.at[0],
            device_id={"tm": part_from[0], "det": part_from[1]},
            device_id_type=MESH,
        ).wait_recv()

    @pl.when(stays)
    def _():
        part_stays.wait()

    each_chip(lambda other: chip_copy(other, chip).start())

    for load in loads[1:]:
        load.wait()
    to_detector.wait_recv()

    to_pair = Exchange("tm", PLANES, 8, CHUNKS, x2, x3, c_send.at[0], c_recv.at[0])
    from_pair = Exchange("tm", PLANES, 8, CHUNKS, x8, x9, c_send.at[1], c_recv.at[1])

    samples_of = split(x1[...])
    for half in range(2):
        parts = []
        for offset in (128 * half, 256 + 128 * half):
            rows = slice(offset, offset + 128)
            parts.append(product((t_first_high[rows], t_first_low[rows]), samples_of, (1, 0)))
        real, imag = parts
        rows = slice(128 * half, 128 * half + 128)
        cos, sin = t_cos[rows], t_sin[rows]
        turned = jnp.concatenate([real * cos + imag * sin, imag * cos - real * sin], axis=1)
        bins = product((t_second_high[...], t_second_low[...]), split(turned), (1, 1))
        for p in range(PLANES):
            x2[32 * p + 16 * half : 32 * p + 16 * half + 16, :] = bins[16 * p : 16 * p + 16]
        to_pair.start(2 * half)
        to_pair.start(2 * half + 1)

    def bins_copy(n, source, target, peer, source_block, target_block, slot):
        return pltpu.make_async_remote_copy(
            src_ref=source.at[rows_at(source_block, 16)],
            dst_ref=target.at[rows_at(target_block, 16)],
            send_sem=d_send.at[n, peer],
            recv_sem=d_recv.at[n, slot],
            device_id={"det": peer},
            device_id_type=MESH,
        )

    def each_group(action):
        def step(k, carry):
            action(lax.rem(group + away(k, GROUPS), GROUPS))
            return carry

        lax.fori_loop(0, GROUPS - 1, step, 0, unroll=True)

    def spread(chunk):
        to_pair.wait_recv(chunk)
        for u in range(8):
            peer = 4 * u + chunk
            x4[rows_at(peer, 16)] = x3[pl.ds(8 * chunk + u, PLANES, stride=32), :]

        def step(u, carry):
            peer = 4 * lax.rem(group // 4 + u + 4, 8) + chunk

            @pl.when(peer != group)
            def _():
                bins_copy(0, x4, x5, peer, peer, group, group).start()

            return carry

        lax.fori_loop(0, 8, step, 0, unroll=True)

        @pl.when(kind == chunk)
        def _():
            x5[rows_at(group, 16)] = x4[rows_at(group, 16)]

    def factor_ready():
        each_chip(lambda other: chip_copy(other, other).wait_recv())
        core_copy(core).start()
        core_copy(1 - core).wait_recv()
        high, low = split(gathered[...].reshape(DETS, DETS))
        factor_high[...] = high
        factor_low[...] = low

    def mix():
        each_group(lambda other: bins_copy(0, x4, x5, other, other, other, other).wait_recv())
        high, low = split(x5[...])
        for quarter in range(4):
            rows = slice(128 * quarter, 128 * quarter + 128)
            depth = 128 * quarter + 128
            x6[rows] = product(
                (factor_high[rows, :depth], factor_low[rows, :depth]), (high[:depth], low[:depth]), (1, 0)
            )

            def step(u, carry):
                peer = 8 * quarter + u

                @pl.when(peer != group)
                def _():
                    bins_copy(1, x6, x7, peer, peer, group, group).start()

                return carry

            lax.fori_loop(0, 8, step, 0, unroll=True)
        x7[rows_at(group, 16)] = x6[rows_at(group, 16)]

    def gather(chunk):
        def step(u, carry):
            other = 4 * u + chunk

            @pl.when(other != group)
            def _():
                bins_copy(1, x6, x7, other, other, other, other).wait_recv()

            return carry

        lax.fori_loop(0, 8, step, 0, unroll=True)
        for u in range(8):
            x8[pl.ds(8 * chunk + u, PLANES, stride=32), :] = x7[rows_at(4 * u + chunk, 16)]
        from_pair.start(chunk)

    factor_ready()

    def stage(n, carry):
        @pl.when(n < CHUNKS)
        def _():
            spread(n)

        @pl.when(kind == n - 1)
        def _():
            mix()

        @pl.when(n >= 2)
        def _():
            gather(n - 2)

        return carry

    lax.fori_loop(0, CHUNKS + 2, stage, 0)

    for half in range(2):
        from_pair.wait_recv(2 * half)
        from_pair.wait_recv(2 * half + 1)
        for p in range(PLANES):
            flat[16 * p : 16 * p + 16] = x9[32 * p + 16 * half : 32 * p + 16 * half + 16, :]
        back = product(split(flat[...]), (t_second_high[...], t_second_low[...]), (0, 0))
        real, imag = back[:, :LANES], back[:, LANES:]
        rows = slice(128 * half, 128 * half + 128)
        cos, sin = t_cos[rows], t_sin[rows]
        for offset, turned in (
            (128 * half, real * cos - imag * sin),
            (256 + 128 * half, imag * cos + real * sin),
        ):
            high, low = split(turned * (2.0 / TOTAL))
            turned_high[offset : offset + 128] = high
            turned_low[offset : offset + 128] = low
    x10[...] = product(
        (t_first_high[...], t_first_low[...]), (turned_high[...], turned_low[...]), (0, 0)
    )

    to_block = Exchange("tm", PLANES, 32, 1, x10, x11, z_send.at[1], z_recv.at[1])
    to_block.start()
    to_block.wait_recv()
    for j in range(32):
        out[:, LANES * j : LANES * (j + 1)] = x11[pl.ds(j, PLANES, stride=32), :]

    @pl.when(leaves)
    def _():
        part_copy.wait_send()

    each_chip(lambda other: chip_copy(other, chip).wait_send())
    core_copy(core).wait_send()
    each_group(lambda other: bins_copy(0, x4, x5, other, other, group, group).wait_send())
    each_group(lambda other: bins_copy(1, x6, x7, other, other, group, group).wait_send())
    for exchange in (to_detector, to_pair, from_pair, to_block):
        exchange.wait_send()


def local(noise, factor):
    any_space = pl.BlockSpec(memory_space=pl.ANY)
    block = pltpu.VMEM((ROWS, LANES), f32)
    return pl.pallas_call(
        kernel,
        out_shape=jax.ShapeDtypeStruct((PLANES, ROWS * LANES // PLANES), f32),
        in_specs=[any_space] * 8,
        out_specs=pl.BlockSpec(memory_space=pltpu.VMEM),
        scratch_shapes=[
            pltpu.VMEM((PLANES, ROWS * LANES // PLANES), f32),
            *[block] * 12,
            pltpu.VMEM((256, LANES), f32),
            pltpu.VMEM((ROWS, LANES), bf16),
            pltpu.VMEM((ROWS, LANES), bf16),
            pltpu.VMEM((16, 32, DETS), f32),
            pltpu.VMEM((DETS, DETS), bf16),
            pltpu.VMEM((DETS, DETS), bf16),
            pltpu.VMEM((512, 512), bf16),
            pltpu.VMEM((512, 512), bf16),
            pltpu.VMEM((256, 256), bf16),
            pltpu.VMEM((256, 256), bf16),
            pltpu.VMEM((256, LANES), f32),
            pltpu.VMEM((256, LANES), f32),
            pltpu.SemaphoreType.DMA((2, PLANES, 1)),
            pltpu.SemaphoreType.DMA((2, PLANES, 1)),
            pltpu.SemaphoreType.DMA((2, PLANES, CHUNKS)),
            pltpu.SemaphoreType.DMA((2, PLANES, CHUNKS)),
            pltpu.SemaphoreType.DMA((2, GROUPS)),
            pltpu.SemaphoreType.DMA((2, GROUPS)),
            pltpu.SemaphoreType.DMA((16,)),
            pltpu.SemaphoreType.DMA((16,)),
            pltpu.SemaphoreType.DMA((2,)),
            pltpu.SemaphoreType.DMA((2,)),
            pltpu.SemaphoreType.DMA((8,)),
        ],
        compiler_params=pltpu.CompilerParams(collective_id=0, has_side_effects=True),
        name="mix",
    )(noise, factor, *make_tables())


def solution(mesh):
    in_specs = (P("det", "tm"), P("det", "tm", None))
    return jax.shard_map(local, mesh=mesh, in_specs=in_specs, out_specs=P("det", "tm"), check_vma=False)
```

time: 102 us -> 92.5 us (0.907); the launches traced: 101 us -> 92.3 us
  Pallas kernels: 98.8 us -> 90.6 us
    pallas_call x1, Pallas kernels: 98.8 us -> 90.6 us  [local(): pl.pallas_call(kernel, out_shape=jax.ShapeDtypeStruct((PLANES, ROWS * LAN...]
where the time goes in v1:
time: 92.5 us; the launch traced here: 92.3 us
  Pallas kernels  90.6 us (98%)
  local copies, waits for them, and re-layouts  1.67 us (2%)
    pallas_call x1, Pallas kernels, local(): pl.pallas_call(kernel, out_shape=jax.ShapeDtypeStruct((PLANES, ROWS * LAN...  90.6 us

profile of v1, /device:TPU:24, one launch (start us, length us, event | category | flops | bytes accessed | tf_op | source)
XLA Modules:
  0.0 92.3 jit_solution(18422578028541221985)
XLA Ops:
  0.0 90.6 %mix.1 = f32[16,4096]{1,0:T(8,128)} custom-call(f32[16,4096]{1,0:T(8,128)} %noise.1, f32[1,32,512]{2,1,0:T(8,128)} %factor.1, bf16[512,512]{1,0:T(8,128)(2,1)} %constant.12.clone.first_high, bf16[512,512]{1,0:T(8,128)(2,1)} %constant.13.clone.first_low, bf16[256,256]{1,0:T(8,128)(2,1)} %constant.14.clone.second_high, ...), custom_call_target="tpu_custom_call" | custom-call | tf_op jit(solution)/shard_map/mix/pallas_call | solution.py:415
  90.6 1.7 %copy.10 = f32[16,4096]{1,0:T(8,128)} copy(f32[16,4096]{1,0:T(8,128)} %mix.1) | data formatting | bytes 524288

commit v2 on v1

--- a/solution.py
+++ b/solution.py
@@ -68,52 +68,46 @@
     return count // 2 + (step + 1) // 2 * (1 - 2 * (step % 2))
 
 
+def await_rows(ref, sem):
+    pltpu.make_async_copy(ref, ref, sem).wait()
+
+
 class Exchange:
     def __init__(self, axis, count, rows, chunks, source, target, send, recv):
         self.axis, self.count, self.rows, self.chunks = axis, count, rows, chunks
         self.source, self.target, self.send, self.recv = source, target, send, recv
 
-    def block(self, ref, index, chunk):
-        return ref.at[rows_at(index * self.chunks + chunk, self.rows)]
-
-    def copy(self, peer, source_block, target_block, slot, chunk):
-        return pltpu.make_async_remote_copy(
-            src_ref=self.block(self.source, source_block, chunk),
-            dst_ref=self.block(self.target, target_block, chunk),
-            send_sem=self.send.at[peer, chunk],
-            recv_sem=self.recv.at[slot, chunk],
-            device_id={self.axis: peer},
-            device_id_type=MESH,
-        )
-
-    def each(self, action):
-        me = lax.axis_index(self.axis)
-
-        def step(k, carry):
-            action(me, lax.rem(me + away(k, self.count), self.count))
-            return carry
-
-        lax.fori_loop(0, self.count - 1, step, 0, unroll=True)
-
     def start(self, chunk=0):
-        self.each(lambda me, peer: self.copy(peer, peer, me, me, chunk).start())
         me = lax.axis_index(self.axis)
         here = rows_at(me * self.chunks + chunk, self.rows)
+
+        def step(k, carry):
+            peer = lax.rem(me + away(k, self.count), self.count)
+            pltpu.make_async_remote_copy(
+                src_ref=self.source.at[rows_at(peer * self.chunks + chunk, self.rows)],
+                dst_ref=self.target.at[here],
+                send_sem=self.send,
+                recv_sem=self.recv.at[chunk],
+                device_id={self.axis: peer},
+                device_id_type=MESH,
+            ).start()
+            return carry
+
+        lax.fori_loop(0, self.count - 1, step, 0, unroll=True)
         self.target[here] = self.source[here]
 
     def wait_recv(self, chunk=0):
-        self.each(lambda me, peer: self.copy(peer, me, peer, peer, chunk).wait_recv())
+        await_rows(self.target.at[0 : (self.count - 1) * self.rows], self.recv.at[chunk])
 
     def wait_send(self):
-        for chunk in range(self.chunks):
-            self.each(lambda me, peer: self.copy(peer, peer, me, me, chunk).wait_send())
+        await_rows(self.source.at[0 : (self.count - 1) * self.rows * self.chunks], self.send)
 
 
 def kernel(
     noise, factor, first_high, first_low, second_high, second_low, cosines, sines, out,
     samples, x0, x1, x2, x3, x4, x5, x6, x7, x8, x9, x10, x11, flat, turned_high, turned_low, gathered, factor_high, factor_low,
     t_first_high, t_first_low, t_second_high, t_second_low, t_cos, t_sin,
-    z_send, z_recv, c_send, c_recv, d_send, d_recv, f_send, f_recv, part_send, part_recv, local_sem,
+    z_send, z_recv, c_send, c_recv, d_send, d_recv, f_send, f_recv, twin_send, twin_recv, part_send, part_recv, local_sem,
 ):
     plane = lax.axis_index("tm")
     group = lax.axis_index("det")
@@ -122,8 +116,10 @@
     chip = group // 2
     kind = lax.rem(group, CHUNKS)
     pair = group + upper * (31 - 2 * group)
-    part_to = (pair, 2 * plane + upper)
-    part_from = (chip, plane + core * (31 - 2 * plane))
+    sent = 2 * plane + upper
+    part_to = (pair, 2 * lax.rem(plane + pair, PLANES) + upper)
+    mine = lax.rem(chip - plane + PLANES, PLANES)
+    part_from = (mine, plane + core * (31 - 2 * plane))
     stays = jnp.logical_and(part_to[0] == plane, part_to[1] == group)
     leaves = jnp.logical_not(stays)
 
@@ -173,78 +169,84 @@
     def _():
         pl.semaphore_wait(barrier, PLANES + GROUPS)
 
+    to_detector = Exchange("tm", PLANES, 32, 1, x0, x1, z_send.at[0], z_recv.at[pl.ds(0, 1)])
+    to_detector.start()
+
     part = factor.at[0, pl.ds(pl.multiple_of(16 * upper, 16), 16)]
 
     def factor_block(index):
         return gathered.at[index // 2, pl.ds(pl.multiple_of(16 * lax.rem(index, 2), 16), 16)]
 
-    part_copy = pltpu.make_async_remote_copy(
-        src_ref=part,
-        dst_ref=factor_block(part_to[1]),
-        send_sem=part_send.at[0],
-        recv_sem=part_recv.at[0],
-        device_id={"tm": part_to[0], "det": part_to[1]},
-        device_id_type=MESH,
-    )
-    part_stays = pltpu.make_async_copy(part, factor_block(group), part_recv.at[0])
+    def part_copy(quarter, index, other):
+        columns = pl.ds(0, 128 * quarter + 128)
+        return pltpu.make_async_remote_copy(
+            src_ref=part.at[:, columns],
+            dst_ref=factor_block(index).at[:, columns],
+            send_sem=part_send,
+            recv_sem=part_recv,
+            device_id={"tm": other[0], "det": other[1]},
+            device_id_type=MESH,
+        )
+
+    part_stays = pltpu.make_async_copy(part, factor_block(sent), part_recv)
+
+    def each_quarter(of, action):
+        for quarter in range(4):
+
+            @pl.when(of // 4 == quarter)
+            def _():
+                action(quarter)
 
     @pl.when(leaves)
     def _():
-        part_copy.start()
+        each_quarter(plane, lambda quarter: part_copy(quarter, sent, part_to).start())
 
     @pl.when(stays)
     def _():
         part_stays.start()
 
-    to_detector = Exchange("tm", PLANES, 32, 1, x0, x1, z_send.at[0], z_recv.at[0])
-    to_detector.start()
-
-    def chip_copy(other, block):
+    def chip_copy(quarter, other, block):
+        columns = pl.ds(0, 128 * quarter + 128)
         return pltpu.make_async_remote_copy(
-            src_ref=factor_block(2 * block + core),
-            dst_ref=factor_block(2 * block + core),
-            send_sem=f_send.at[other],
+            src_ref=factor_block(2 * block + core).at[:, columns],
+            dst_ref=factor_block(2 * block + core).at[:, columns],
+            send_sem=f_send,
             recv_sem=f_recv.at[block],
             device_id={"det": 2 * other + core},
             device_id_type=MESH,
         )
 
-    def each_chip(action):
+    def to_chips(quarter):
         def step(k, carry):
-            action(lax.rem(chip + away(k, 16), 16))
+            chip_copy(quarter, lax.rem(chip + away(k, 16), 16), mine).start()
             return carry
 
-        lax.fori_loop(0, 15, step, 0, unroll=True)
-
-    def half_of(index):
-        return gathered.at[:, pl.ds(pl.multiple_of(16 * index, 16), 16)]
-
-    def core_copy(half):
+        lax.fori_loop(0, 15, step, 0)
+
+    def core_copy(half, quarter):
+        ref = gathered.at[
+            4 * quarter : 4 * quarter + 4,
+            pl.ds(pl.multiple_of(16 * half, 16), 16),
+            0 : 128 * quarter + 128,
+        ]
         return pltpu.make_async_remote_copy(
-            src_ref=half_of(half),
-            dst_ref=half_of(half),
-            send_sem=part_send.at[1],
-            recv_sem=part_recv.at[1],
+            src_ref=ref,
+            dst_ref=ref,
+            send_sem=twin_send.at[quarter],
+            recv_sem=twin_recv.at[quarter],
             device_id={"det": group + 1 - 2 * core},
             device_id_type=MESH,
         )
 
-    @pl.when(leaves)
-    def _():
-        pltpu.make_async_remote_copy(
-            src_ref=part,
-            dst_ref=factor_block(group),
-            send_sem=part_send.at[0],
-            recv_sem=part_recv.at[0],
-            device_id={"tm": part_from[0], "det": part_from[1]},
-            device_id_type=MESH,
-        ).wait_recv()
-
-    @pl.when(stays)
-    def _():
-        part_stays.wait()
-
-    each_chip(lambda other: chip_copy(other, chip).start())
+    def to_core():
+        for quarter in range(4):
+            for block in range(4 * quarter, 4 * quarter + 4):
+
+                @pl.when(block != mine)
+                def _():
+                    chip_copy(quarter, chip, block).wait_recv()
+
+            core_copy(core, quarter).start()
 
     for load in loads[1:]:
         load.wait()
@@ -269,54 +271,54 @@
         to_pair.start(2 * half)
         to_pair.start(2 * half + 1)
 
-    def bins_copy(n, source, target, peer, source_block, target_block, slot):
-        return pltpu.make_async_remote_copy(
-            src_ref=source.at[rows_at(source_block, 16)],
-            dst_ref=target.at[rows_at(target_block, 16)],
-            send_sem=d_send.at[n, peer],
-            recv_sem=d_recv.at[n, slot],
+    @pl.when(leaves)
+    def _():
+        each_quarter(mine, lambda quarter: part_copy(quarter, sent, part_from).wait_recv())
+
+    @pl.when(stays)
+    def _():
+        part_stays.wait()
+
+    each_quarter(mine, to_chips)
+
+    def bins_copy(n, source, target, peer):
+        pltpu.make_async_remote_copy(
+            src_ref=source.at[rows_at(peer, 16)],
+            dst_ref=target.at[rows_at(group, 16)],
+            send_sem=d_send.at[n],
+            recv_sem=d_recv.at[n * CHUNKS + (kind if n else 0)],
             device_id={"det": peer},
             device_id_type=MESH,
-        )
-
-    def each_group(action):
-        def step(k, carry):
-            action(lax.rem(group + away(k, GROUPS), GROUPS))
-            return carry
-
-        lax.fori_loop(0, GROUPS - 1, step, 0, unroll=True)
+        ).start()
 
     def spread(chunk):
         to_pair.wait_recv(chunk)
         for u in range(8):
-            peer = 4 * u + chunk
-            x4[rows_at(peer, 16)] = x3[pl.ds(8 * chunk + u, PLANES, stride=32), :]
-
-        def step(u, carry):
-            peer = 4 * lax.rem(group // 4 + u + 4, 8) + chunk
-
-            @pl.when(peer != group)
-            def _():
-                bins_copy(0, x4, x5, peer, peer, group, group).start()
-
-            return carry
-
-        lax.fori_loop(0, 8, step, 0, unroll=True)
+            x4[rows_at(4 * u + chunk, 16)] = x3[pl.ds(8 * chunk + u, PLANES, stride=32), :]
+
+        for u in (4, 3, 5, 2, 6, 1, 7):
+            bins_copy(0, x4, x5, 4 * lax.rem(group // 4 + u, 8) + chunk)
+
+        @pl.when(kind != chunk)
+        def _():
+            bins_copy(0, x4, x5, 4 * (group // 4) + chunk)
 
         @pl.when(kind == chunk)
         def _():
             x5[rows_at(group, 16)] = x4[rows_at(group, 16)]
 
     def factor_ready():
-        each_chip(lambda other: chip_copy(other, other).wait_recv())
-        core_copy(core).start()
-        core_copy(1 - core).wait_recv()
-        high, low = split(gathered[...].reshape(DETS, DETS))
-        factor_high[...] = high
-        factor_low[...] = low
+        for quarter in range(4):
+            core_copy(1 - core, quarter).wait_recv()
+            rows = slice(128 * quarter, 128 * quarter + 128)
+            depth = 128 * quarter + 128
+            block = gathered[4 * quarter : 4 * quarter + 4, :, :depth]
+            high, low = split(block.reshape(128, depth))
+            factor_high[rows, :depth] = high
+            factor_low[rows, :depth] = low
 
     def mix():
-        each_group(lambda other: bins_copy(0, x4, x5, other, other, other, other).wait_recv())
+        await_rows(x5.at[0 : DETS - 16], d_recv.at[0])
         high, low = split(x5[...])
         for quarter in range(4):
             rows = slice(128 * quarter, 128 * quarter + 128)
@@ -324,52 +326,52 @@
             x6[rows] = product(
                 (factor_high[rows, :depth], factor_low[rows, :depth]), (high[:depth], low[:depth]), (1, 0)
             )
-
-            def step(u, carry):
-                peer = 8 * quarter + u
-
-                @pl.when(peer != group)
-                def _():
-                    bins_copy(1, x6, x7, peer, peer, group, group).start()
-
-                return carry
-
-            lax.fori_loop(0, 8, step, 0, unroll=True)
+            for u in range(1, 8):
+                bins_copy(1, x6, x7, 8 * quarter + lax.rem(group + u, 8))
+
+            @pl.when(group // 8 != quarter)
+            def _():
+                bins_copy(1, x6, x7, 8 * quarter + lax.rem(group, 8))
+
         x7[rows_at(group, 16)] = x6[rows_at(group, 16)]
 
     def gather(chunk):
-        def step(u, carry):
-            other = 4 * u + chunk
-
-            @pl.when(other != group)
-            def _():
-                bins_copy(1, x6, x7, other, other, other, other).wait_recv()
-
-            return carry
-
-        lax.fori_loop(0, 8, step, 0, unroll=True)
+        @pl.when(kind == chunk)
+        def _():
+            await_rows(x7.at[0:112], d_recv.at[CHUNKS + chunk])
+
+        @pl.when(kind != chunk)
+        def _():
+            await_rows(x7.at[0:128], d_recv.at[CHUNKS + chunk])
+
         for u in range(8):
             x8[pl.ds(8 * chunk + u, PLANES, stride=32), :] = x7[rows_at(4 * u + chunk, 16)]
         from_pair.start(chunk)
 
-    factor_ready()
-
     def stage(n, carry):
         @pl.when(n < CHUNKS)
         def _():
             spread(n)
 
+        @pl.when(n == 0)
+        def _():
+            to_core()
+
+        @pl.when(n == 1)
+        def _():
+            factor_ready()
+
         @pl.when(kind == n - 1)
         def _():
             mix()
 
-        @pl.when(n >= 2)
-        def _():
-            gather(n - 2)
+        @pl.when(n >= 3)
+        def _():
+            gather(n - 3)
 
         return carry
 
-    lax.fori_loop(0, CHUNKS + 2, stage, 0)
+    lax.fori_loop(0, CHUNKS + 3, stage, 0)
 
     for half in range(2):
         from_pair.wait_recv(2 * half)
@@ -391,7 +393,7 @@
         (t_first_high[...], t_first_low[...]), (turned_high[...], turned_low[...]), (0, 0)
     )
 
-    to_block = Exchange("tm", PLANES, 32, 1, x10, x11, z_send.at[1], z_recv.at[1])
+    to_block = Exchange("tm", PLANES, 32, 1, x10, x11, z_send.at[1], z_recv.at[pl.ds(1, 1)])
     to_block.start()
     to_block.wait_recv()
     for j in range(32):
@@ -399,12 +401,15 @@
 
     @pl.when(leaves)
     def _():
-        part_copy.wait_send()
-
-    each_chip(lambda other: chip_copy(other, chip).wait_send())
-    core_copy(core).wait_send()
-    each_group(lambda other: bins_copy(0, x4, x5, other, other, group, group).wait_send())
-    each_group(lambda other: bins_copy(1, x6, x7, other, other, group, group).wait_send())
+        each_quarter(plane, lambda quarter: part_copy(quarter, sent, part_to).wait_send())
+
+    each_quarter(
+        mine, lambda quarter: await_rows(gathered.at[0:15, 0:16, 0 : 128 * quarter + 128], f_send)
+    )
+    for quarter in range(4):
+        core_copy(core, quarter).wait_send()
+    await_rows(x4.at[0 : DETS - 16], d_send.at[0])
+    await_rows(x6.at[0 : DETS - 16], d_send.at[1])
     for exchange in (to_detector, to_pair, from_pair, to_block):
         exchange.wait_send()
 
@@ -432,16 +437,18 @@
             pltpu.VMEM((256, 256), bf16),
             pltpu.VMEM((256, LANES), f32),
             pltpu.VMEM((256, LANES), f32),
-            pltpu.SemaphoreType.DMA((2, PLANES, 1)),
-            pltpu.SemaphoreType.DMA((2, PLANES, 1)),
-            pltpu.SemaphoreType.DMA((2, PLANES, CHUNKS)),
-            pltpu.SemaphoreType.DMA((2, PLANES, CHUNKS)),
-            pltpu.SemaphoreType.DMA((2, GROUPS)),
-            pltpu.SemaphoreType.DMA((2, GROUPS)),
-            pltpu.SemaphoreType.DMA((16,)),
-            pltpu.SemaphoreType.DMA((16,)),
             pltpu.SemaphoreType.DMA((2,)),
             pltpu.SemaphoreType.DMA((2,)),
+            pltpu.SemaphoreType.DMA((2,)),
+            pltpu.SemaphoreType.DMA((2, CHUNKS)),
+            pltpu.SemaphoreType.DMA((2,)),
+            pltpu.SemaphoreType.DMA((2 * CHUNKS,)),
+            pltpu.SemaphoreType.DMA,
+            pltpu.SemaphoreType.DMA((16,)),
+            pltpu.SemaphoreType.DMA((4,)),
+            pltpu.SemaphoreType.DMA((4,)),
+            pltpu.SemaphoreType.DMA,
+            pltpu.SemaphoreType.DMA,
             pltpu.SemaphoreType.DMA((8,)),
         ],
         compiler_params=pltpu.CompilerParams(collective_id=0, has_side_effects=True),

time: 92.5 us -> 84.2 us (0.910)
  Pallas kernels: 90.6 us -> 81.5 us
    pallas_call x1, Pallas kernels: 90.6 us -> 81.5 us  [local(): pl.pallas_call(kernel, out_shape=jax.ShapeDtypeStruct((PLANES, ROWS * LAN...]
where the time goes in v2:
time: 84.2 us; the launch traced here: 83.1 us
  Pallas kernels  81.5 us (97%)
  local copies, waits for them, and re-layouts  1.67 us (2%)
    pallas_call x1, Pallas kernels, local(): pl.pallas_call(kernel, out_shape=jax.ShapeDtypeStruct((PLANES, ROWS * LAN...  81.5 us

profile of v2, /device:TPU:24, one launch (start us, length us, event | category | flops | bytes accessed | tf_op | source)
XLA Modules:
  0.0 83.1 jit_solution(2946771151300001768)
XLA Ops:
  0.0 81.5 %mix.1 = f32[16,4096]{1,0:T(8,128)} custom-call(f32[16,4096]{1,0:T(8,128)} %noise.1, f32[1,32,512]{2,1,0:T(8,128)} %factor.1, bf16[512,512]{1,0:T(8,128)(2,1)} %constant.12.clone.first_high, bf16[512,512]{1,0:T(8,128)(2,1)} %constant.13.clone.first_low, bf16[256,256]{1,0:T(8,128)(2,1)} %constant.14.clone.second_high, ...), custom_call_target="tpu_custom_call" | custom-call | tf_op jit(solution)/shard_map/mix/pallas_call | solution.py:420
  81.5 1.7 %copy.10 = f32[16,4096]{1,0:T(8,128)} copy(f32[16,4096]{1,0:T(8,128)} %mix.1) | data formatting | bytes 524288

commit v3 on v2

--- a/solution.py
+++ b/solution.py
@@ -96,6 +96,17 @@
         lax.fori_loop(0, self.count - 1, step, 0, unroll=True)
         self.target[here] = self.source[here]
 
+    def send_to(self, peer):
+        me = lax.axis_index(self.axis)
+        pltpu.make_async_remote_copy(
+            src_ref=self.source.at[rows_at(peer, self.rows)],
+            dst_ref=self.target.at[rows_at(me, self.rows)],
+            send_sem=self.send,
+            recv_sem=self.recv.at[0],
+            device_id={self.axis: peer},
+            device_id_type=MESH,
+        ).start()
+
     def wait_recv(self, chunk=0):
         await_rows(self.target.at[0 : (self.count - 1) * self.rows], self.recv.at[chunk])
 
@@ -365,13 +376,13 @@
         def _():
             mix()
 
-        @pl.when(n >= 3)
-        def _():
-            gather(n - 3)
+        @pl.when(n >= 2)
+        def _():
+            gather(n - 2)
 
         return carry
 
-    lax.fori_loop(0, CHUNKS + 3, stage, 0)
+    lax.fori_loop(0, CHUNKS + 2, stage, 0)
 
     for half in range(2):
         from_pair.wait_recv(2 * half)
@@ -389,12 +400,18 @@
             high, low = split(turned * (2.0 / TOTAL))
             turned_high[offset : offset + 128] = high
             turned_low[offset : offset + 128] = low
-    x10[...] = product(
-        (t_first_high[...], t_first_low[...]), (turned_high[...], turned_low[...]), (0, 0)
-    )
-
     to_block = Exchange("tm", PLANES, 32, 1, x10, x11, z_send.at[1], z_recv.at[pl.ds(1, 1)])
-    to_block.start()
+    turned = (turned_high[...], turned_low[...])
+    for step in (2, 1, 3, 0):
+        quarter = lax.rem(plane // 4 + step, 4)
+        columns = pl.ds(pl.multiple_of(LANES * quarter, LANES), LANES)
+        x10[rows_at(quarter, LANES)] = product(
+            (t_first_high[:, columns], t_first_low[:, columns]), turned, (0, 0)
+        )
+        for place in (2, 1, 3, 0):
+            if step or place:
+                to_block.send_to(4 * quarter + lax.rem(plane + place, 4))
+    x11[rows_at(plane, 32)] = x10[rows_at(plane, 32)]
     to_block.wait_recv()
     for j in range(32):
         out[:, LANES * j : LANES * (j + 1)] = x11[pl.ds(j, PLANES, stride=32), :]

time: 84.2 us -> 83.9 us (level); the launches traced: 83.1 us -> 83.8 us
  no operation moved by 1% of the time
where the time goes in v3:
time: 83.9 us; the launch traced here: 83.8 us
  Pallas kernels  82.1 us (98%)
  local copies, waits for them, and re-layouts  1.67 us (2%)
    pallas_call x1, Pallas kernels, local(): pl.pallas_call(kernel, out_shape=jax.ShapeDtypeStruct((PLANES, ROWS * LAN...  82.1 us

profile of v3, /device:TPU:24, one launch (start us, length us, event | category | flops | bytes accessed | tf_op | source)
XLA Modules:
  0.0 83.8 jit_solution(17475883622012380320)
XLA Ops:
  0.0 82.1 %mix.1 = f32[16,4096]{1,0:T(8,128)} custom-call(f32[16,4096]{1,0:T(8,128)} %noise.1, f32[1,32,512]{2,1,0:T(8,128)} %factor.1, bf16[512,512]{1,0:T(8,128)(2,1)} %constant.12.clone.first_high, bf16[512,512]{1,0:T(8,128)(2,1)} %constant.13.clone.first_low, bf16[256,256]{1,0:T(8,128)(2,1)} %constant.14.clone.second_high, ...), custom_call_target="tpu_custom_call" | custom-call | tf_op jit(solution)/shard_map/mix/pallas_call | solution.py:437
  82.1 1.7 %copy.10 = f32[16,4096]{1,0:T(8,128)} copy(f32[16,4096]{1,0:T(8,128)} %mix.1) | data formatting | bytes 524288

commit v4 on v2

--- a/solution.py
+++ b/solution.py
@@ -365,13 +365,13 @@
         def _():
             mix()
 
-        @pl.when(n >= 3)
-        def _():
-            gather(n - 3)
+        @pl.when(n >= 2)
+        def _():
+            gather(n - 2)
 
         return carry
 
-    lax.fori_loop(0, CHUNKS + 3, stage, 0)
+    lax.fori_loop(0, CHUNKS + 2, stage, 0)
 
     for half in range(2):
         from_pair.wait_recv(2 * half)

time: 84.2 us -> 83.7 us (level); the launches traced: 83.1 us -> 83.5 us
  no operation moved by 1% of the time
where the time goes in v4:
time: 83.7 us; the launch traced here: 83.5 us
  Pallas kernels  81.9 us (98%)
  local copies, waits for them, and re-layouts  1.67 us (2%)
    pallas_call x1, Pallas kernels, local(): pl.pallas_call(kernel, out_shape=jax.ShapeDtypeStruct((PLANES, ROWS * LAN...  81.9 us

profile of v4, /device:TPU:24, one launch (start us, length us, event | category | flops | bytes accessed | tf_op | source)
XLA Modules:
  0.0 83.5 jit_solution(6463132554514059133)
XLA Ops:
  0.0 81.9 %mix.1 = f32[16,4096]{1,0:T(8,128)} custom-call(f32[16,4096]{1,0:T(8,128)} %noise.1, f32[1,32,512]{2,1,0:T(8,128)} %factor.1, bf16[512,512]{1,0:T(8,128)(2,1)} %constant.12.clone.first_high, bf16[512,512]{1,0:T(8,128)(2,1)} %constant.13.clone.first_low, bf16[256,256]{1,0:T(8,128)(2,1)} %constant.14.clone.second_high, ...), custom_call_target="tpu_custom_call" | custom-call | tf_op jit(solution)/shard_map/mix/pallas_call | solution.py:420
  81.9 1.7 %copy.10 = f32[16,4096]{1,0:T(8,128)} copy(f32[16,4096]{1,0:T(8,128)} %mix.1) | data formatting | bytes 524288
